TPU v7x, 32 devices: a whole 2x2x4 slice. The times are simulated.
32 devices in a mesh: seg: 2 (over y), chan: 8 (over z, core), tm: 2 (over x).
Axes of the slice: x: 2, y: 2, z: 4, core: 2. Of those that a mesh axis runs over, the one named last changes fastest.
Arguments:
- traces: bfloat16 [1024, 12288], P(('seg', 'chan'), 'tm'), parts along dimension 0, may hold values from -14 to 14
- filter_taps: float32 [512, 33], P('chan'), may hold values from -1 to 1
- source_counts: int32 [8], replicated, may hold values from 1 to 36, 96 in all
- source_channel: int32 [8, 36], replicated, may hold values from 0 to 63
- block_sources: int32 [8, 12], P('chan'), may hold values from 0 to 95
Outputs:
- stacked: float32 [1024, 12, 1024], P(('seg', 'chan', 'tm')), parts along dimension 0
There are 2 independent parts, one for each index of `seg`. A program takes and returns all parts, laid end to end along the dimension named above; an argument that names none is the same for every part. Nothing has to cross between parts.
Inputs may be any that keep to these rules, and one draw needn't show every extreme that they name: `source_counts`: the entries sum to 96 and the largest is exactly 36. `source_channel`: only the first source_counts[h] entries of row h name virtual sources.
All inputs are finite; a program needn't handle non-finite values.
Results may differ from a plain program's by a relative error of at most 0.0072.
Values may be sent and summed in bfloat16 or wider, within the bound.
No kernel may reach another device: no remote copies, remote signals or barrier semaphores. Data moves between devices by JAX's collectives and lax.ppermute only.
A program may use at most 64 MiB of HBM per device.

v0:
```python
import math
import jax
import jax.numpy as jnp
from jax import lax
from jax.sharding import PartitionSpec as P

TILE = 64
NFFT = 4096
NF = 512
F0 = 8


def from_behind(block, axis, distance):
    devices = range(lax.axis_size(axis))
    route = [(i - distance, i) for i in devices if i - distance in devices]
    return lax.ppermute(block, axis, route)


def transform_table():
    sample_index = jnp.arange(NFFT, dtype=jnp.int32)[:, None]
    frequency = F0 + jnp.arange(NF, dtype=jnp.int32)[None, :]
    phase_index = frequency * sample_index % NFFT
    angles = phase_index.astype(jnp.float32) * jnp.float32(2.0 * math.pi / NFFT)
    cosine = jnp.cos(angles).astype(jnp.bfloat16)
    sine_part = (-jnp.sin(angles)).astype(jnp.bfloat16)
    return jnp.concatenate([cosine, sine_part], axis=1)


def apply_filter(extended, filter_taps):
    tap_count = filter_taps.shape[1]
    length = extended.shape[1] - (tap_count - 1)
    summed = jnp.zeros((extended.shape[0], length), jnp.float32)
    for tap_index in range(tap_count):
        first_sample = tap_count - 1 - tap_index
        summed = (
            summed
            + filter_taps[:, tap_index : tap_index + 1]
            * extended[:, first_sample : first_sample + length]
        )
    return summed.astype(jnp.bfloat16)


def intersecting(filtered, hop_length):
    channel_count = filtered.shape[0]
    pieces = filtered.reshape(channel_count, -1, hop_length)
    return jnp.concatenate([pieces[:, :-1], pieces[:, 1:]], axis=2)


def whiten(spectra):
    half_width = spectra.shape[-1] // 2
    real_part = spectra[..., :half_width]
    imag_part = spectra[..., half_width:]
    powers = real_part * real_part + imag_part * imag_part
    widths = [(0, 0)] * (powers.ndim - 1) + [(2, 2)]
    padded = jnp.pad(powers, widths)
    smooth = (
        padded[..., 0:half_width]
        + padded[..., 1 : half_width + 1]
        + padded[..., 2 : half_width + 2]
        + padded[..., 3 : half_width + 3]
        + padded[..., 4 : half_width + 4]
    ) / 5.0
    mean_power = jnp.mean(powers, axis=-1, keepdims=True)
    scaling = lax.rsqrt(smooth + 0.1 * mean_power + 1e-06)
    return jnp.concatenate([real_part * scaling, imag_part * scaling], axis=-1).astype(jnp.bfloat16)


def correlate(receivers, sources, factor):
    half_width = receivers.shape[-1] // 2
    receiver_real = receivers[..., :half_width]
    receiver_imag = receivers[..., half_width:]
    source_real = sources[..., :half_width]
    source_imag = sources[..., half_width:]
    real_sum = jnp.sum(source_real * receiver_real + source_imag * receiver_imag, axis=-2)
    imag_sum = jnp.sum(source_real * receiver_imag - source_imag * receiver_real, axis=-2)
    return jnp.concatenate([real_sum, imag_sum], axis=-1) * factor


def source_rows(source_counts, source_channel, wanted):
    offsets = jnp.cumsum(source_counts) - source_counts
    home_group = jnp.sum((wanted[..., None] >= offsets).astype(jnp.int32), axis=-1) - 1
    slot_index = wanted - offsets[home_group]
    local_channel = source_channel[home_group, slot_index]
    return (home_group, slot_index, local_channel)


def shards(traces, filter_taps, source_counts, source_channel, block_sources):
    channels_here, samples_here = traces.shape
    tap_count = filter_taps.shape[1]
    hop_length = NFFT // 2
    halo_width = hop_length + tap_count - 1
    tail_samples = from_behind(traces[:, samples_here - halo_width :], "tm", 1)
    extended = jnp.concatenate([tail_samples, traces], axis=1).astype(jnp.float32)
    filtered = apply_filter(extended, filter_taps)
    windows_here = samples_here // hop_length
    windows = intersecting(filtered, hop_length).reshape(channels_here * windows_here, NFFT)
    spectra = jnp.dot(windows, transform_table(), preferred_element_type=jnp.float32)
    whitened = whiten(spectra).reshape(channels_here, windows_here, 2 * NF)
    home_group, slot_index, local_channel = source_rows(
        source_counts, source_channel, block_sources
    )
    slot_count = source_channel.shape[1]
    group_index = lax.axis_index("chan")
    own_slots = source_channel[group_index]
    slot_rows = whitened[own_slots]
    everything = lax.all_gather(slot_rows, "chan", axis=0, tiled=True)
    picked = everything[home_group * slot_count + slot_index]
    time_groups = lax.axis_size("tm")
    factor = 1.0 / (windows_here * time_groups)
    receivers = whitened.astype(jnp.float32)
    tile_of_row = (
        jnp.arange(channels_here // time_groups * lax.axis_size("tm"), dtype=jnp.int32) // TILE
    )
    sources = picked[tile_of_row].astype(jnp.float32)
    return lax.psum_scatter(
        correlate(receivers[:, None], sources, factor), "tm", scatter_dimension=0, tiled=True
    )


def solution(mesh):
    in_specs = (P(("seg", "chan"), "tm"), P("chan", None), P(), P(), P("chan", None))
    out_specs = P(("seg", "chan", "tm"), None, None)
    return jax.shard_map(shards, mesh=mesh, in_specs=in_specs, out_specs=out_specs, check_vma=False)
```

profile of v0, /device:TPU:0, one launch (start us, length us, event | category | flops | bytes accessed | tf_op | source)
XLA Modules:
  0.0 170.6 jit_solution(2282567406715070541)
XLA Ops:
  6.5 1.1 slice.239
  7.6 4.9 %collective-permute-start = (bf16[64,2080]{1,0:T(8,128)(2,1)S(1)}, bf16[64,2080]{1,0:T(8,128)(2,1)S(1)}, u32[]{:S(2)}, u32[]{:S(2)}) collective-permute-start(bf16[64,2080]{1,0:T(8,128)(2,1)S(1)} %slice.239), channel_id=1, source_target_pairs={{0,1},{2,3},{4,5},{6,7},{8,9},{10,11},{12,13},{14,15},{16,17},{18,... | collective-permute-start | bytes 798728 | tf_op jit(solution)/shard_map/ppermute | solution.py:16
  12.5 1.0 slice_bitcast_fusion.33
  13.5 35.0 %cosine_convert_fusion = (bf16[4096,512]{1,0:T(8,128)(2,1)}, bf16[4096,512]{1,0:T(8,128)(2,1)}) fusion(s32[512]{0:T(512)S(1)} %iota_add_fusion), kind=kLoop, calls=%fused_computation.14 | loop fusion | flops 35651584 | bytes 8390656 | tf_op jit(solution)/shard_map/convert_element_type | solution.py:24
  48.6 0.7 fusion.51
  49.3 1.0 slice_bitcast_fusion.34
  50.3 0.3 maximum_convert_fusion
  50.6 18.0 %fusion.11 = bf16[64,8192]{1,0:T(8,128)(2,1)S(1)} fusion(f32[64,8224]{1,0:T(8,128)S(1)} %maximum_convert_fusion, f32[64]{0:T(128)S(1)} %get-tuple-element.48, f32[64]{0:T(128)S(1)} %get-tuple-element.49, f32[64]{0:T(128)S(1)} %get-tuple-element.18, f32[64]{0:T(128)S(1)} %get-tuple-element.19, f32[64]{0:T(128)S(1)} %get-tuple-element.20, ...), kind=kLoop, calls=%fused_computation.23 | loop fusion | flops 34603008 | bytes 70263040 | tf_op jit(solution)/shard_map/convert_element_type | solution.py:40
  68.5 0.8 reshape.253
  69.4 1.3 fusion.58
  70.6 1.5 pad_maximum_fusion
  72.1 2.5 %reshape.254 = bf16[192,4096]{1,0:T(8,128)(2,1)} reshape(bf16[64,3,4096]{2,1,0:T(4,128)(2,1)S(1)} %pad_maximum_fusion) | data formatting | bytes 3145728 | tf_op jit(solution)/shard_map/reshape | solution.py:96
  74.6 5.7 %fusion.3 = f32[192,1024]{1,0:T(8,128)S(1)} fusion(bf16[192,4096]{1,0:T(8,128)(2,1)} %reshape.254, bf16[4096,512]{1,0:T(8,128)(2,1)} %get-tuple-element.51, bf16[4096,512]{1,0:T(8,128)(2,1)} %get-tuple-element.50), kind=kOutput, calls=%fused_computation.9 | convolution fusion | flops 1627389952 | bytes 10747904 | tf_op jit(solution)/shard_map/dot_general | solution.py:97
  80.3 0.1 fusion.57
  80.5 0.5 multiply_convert_fusion.1
  81.1 0.1 concatenate.39
  81.2 0.1 concatenate.38
  81.3 0.2 pad_maximum_fusion.1
  81.5 1.6 gather_fusion
  83.2 0.2 reduce-window.9
  83.5 0.7 gather_fusion.1
  84.2 0.1 concatenate.42
  84.3 0.1 concatenate.41
  84.4 0.3 maximum_convert_fusion.1
  84.7 0.2 slice_bitcast_fusion.1
  84.9 0.1 copy.6
  85.1 0.1 copy.7
  85.2 29.9 %all-gather.3.cloned.1.call-done = bf16[288,3,1024]{2,1,0:T(4,128)(2,1)} async-done(((bf16[36,3,1024]{2,1,0:T(4,128)(2,1)}), bf16[288,3,1024]{2,1,0:T(4,128)(2,1)}) %all-gather.3.cloned.1.call-update) | async-done | bytes 1769488 | tf_op jit(solution)/shard_map/all_gather | solution.py:106
  115.1 2.3 %gather_fusion.2 = bf16[12,3,1024]{2,1,0:T(4,128)(2,1)S(1)} fusion(bf16[288,3,1024]{2,1,0:T(4,128)(2,1)} %all-gather.3.cloned.1.call-done, s32[1024]{0:T(1024)S(1)} %pad_clamp_fusion), kind=kCustom, calls=%fused_computation.2 | custom fusion | bytes 147504 | tf_op jit(solution)/shard_map/gather | solution.py:107
  117.4 1.5 add_reduce_fusion
  118.9 2.1 %maximum_multiply_fusion = f32[64,12,1024]{2,0,1:T(8,128)} fusion(f32[64,12,512]{2,0,1:T(8,128)S(1)} %get-tuple-element.6, f32[64,12,512]{2,0,1:T(8,128)S(1)} %get-tuple-element.5), kind=kLoop, calls=%fused_computation.20 | loop fusion | flops 1572864 | bytes 6291456 | tf_op jit(solution)/shard_map/mul | solution.py:76
  121.0 42.8 %reduce-scatter.2.cloned.1.call-done = f32[32,12,1024]{2,0,1:T(8,128)} async-done(((f32[64,12,1024]{2,0,1:T(8,128)}), f32[32,12,1024]{2,0,1:T(8,128)}) %reduce-scatter.2.cloned.1.call-update) | async-done | bytes 1572880 | tf_op jit(solution)/shard_map/reduce_scatter | solution.py:115
  (22 shorter events, 0.3 us)
Async XLA Ops:
  6.5 108.5 %all-gather.3.cloned.1.call-start = ((), (), s32[]{:S(2)}) async-start(), calls=%async_computation.2 | async-start | bytes 2654208 | tf_op jit(solution)/shard_map/all_gather | solution.py:106
  7.6 42.6 %collective-permute-start = (bf16[64,2080]{1,0:T(8,128)(2,1)S(1)}, bf16[64,2080]{1,0:T(8,128)(2,1)S(1)}, u32[]{:S(2)}, u32[]{:S(2)}) collective-permute-start(bf16[64,2080]{1,0:T(8,128)(2,1)S(1)} %slice.239), channel_id=1, source_target_pairs={{0,1},{2,3},{4,5},{6,7},{8,9},{10,11},{12,13},{14,15},{16,17},{18,... | collective-permute-start | bytes 798728 | tf_op jit(solution)/shard_map/ppermute | solution.py:16
  13.5 36.8 %copy-start = (bf16[64,6144]{1,0:T(8,128)(2,1)S(1)}, bf16[64,6144]{1,0:T(8,128)(2,1)}, u32[]{:S(2)}) copy-start(bf16[64,6144]{1,0:T(8,128)(2,1)} %param.5) | copy-start | bytes 2359300
  81.0 2.2 %copy-start.2 = (s32[8]{0:T(128)S(1)}, s32[8]{0:T(128)}, u32[]{:S(2)}) copy-start(s32[8]{0:T(128)} %param.7) | copy-start | bytes 100
  81.0 2.4 %copy-start.1 = (s32[1,12]{1,0:T(1,128)S(1)}, s32[1,12]{1,0:T(1,128)}, u32[]{:S(2)}) copy-start(s32[1,12]{1,0:T(1,128)} %param.9) | copy-start | bytes 148
  83.1 80.7 %reduce-scatter.2.cloned.1.call-start = ((), (), s32[]{:S(2)}) async-start(), calls=%async_computation.1 | async-start | bytes 4718592 | tf_op jit(solution)/shard_map/reduce_scatter | solution.py:115
Sparse Core Ops, SparseCore 0:
  83.3 31.7 all-gather.2
  121.1 42.6 reduce-scatter.1
where the time goes:
time: 171 us
  waiting for transfers between devices  72.8 us (43%)
  other arithmetic  60.5 us (35%)
  between operations  13.6 us (8%)
  local copies, waits for them, and re-layouts  13.1 us (8%)
  matrix products  5.69 us (3%)
  starting transfers between devices  4.93 us (3%)
    reduce_scatter x1, waiting for transfers between devices, shards(): lax.psum_scatter(correlate(receivers[:, None], sources, factor), 'tm', sc...  42.8 us
    convert_element_type x1, other arithmetic, transform_table(): cosine = jnp.cos(angles).astype(jnp.bfloat16)  35 us
    all_gather x1, waiting for transfers between devices, shards(): everything = lax.all_gather(slot_rows, 'chan', axis=0, tiled=True)  29.9 us
    convert_element_type x1, other arithmetic, apply_filter(): return summed.astype(jnp.bfloat16)  18 us
    dot_general x1, matrix products, shards(): jnp.dot(windows, transform_table(), preferred_element_type=jnp.float32)  5.69 us
    ppermute x1, starting transfers between devices, from_behind(): return lax.ppermute(block, axis, route)  4.89 us
  transfers between devices with their start and end apart: 3, of which 2 were waited for; matrix products, arithmetic and copies ran while one was open for 23% of the time, Pallas kernels for 0%

commit v1 on v0

--- a/solution.py
+++ b/solution.py
@@ -103,7 +103,9 @@
     group_index = lax.axis_index("chan")
     own_slots = source_channel[group_index]
     slot_rows = whitened[own_slots]
-    everything = lax.all_gather(slot_rows, "chan", axis=0, tiled=True)
+    u_next = jnp.stack([slot_rows] * lax.axis_size("chan"))
+    r2 = lax.all_to_all(u_next, axis_name="chan", split_axis=0, concat_axis=0)
+    everything = jnp.concatenate(r2, 0)
     picked = everything[home_group * slot_count + slot_index]
     time_groups = lax.axis_size("tm")
     factor = 1.0 / (windows_here * time_groups)

time: 171 us -> 193 us (1.13)
  waiting for transfers between devices: 72.8 us -> 85.8 us
  starting transfers between devices: 4.93 us -> 9.93 us
  local copies, waits for them, and re-layouts: 13.1 us -> 16.9 us
    all_to_all x0 -> x1, waiting for transfers between devices: none -> 44.2 us  [shards(): r2 = lax.all_to_all(u_next, axis_name='chan', split_axis=0, concat_axis=0)]
    all_gather x1 -> x0, waiting for transfers between devices: 29.9 us -> none  [shards(): everything = lax.all_gather(slot_rows, 'chan', axis=0, tiled=True)]
    all_to_all x0 -> x1, starting transfers between devices: none -> 5.01 us  [shards(): r2 = lax.all_to_all(u_next, axis_name='chan', split_axis=0, concat_axis=0)]
    reshape x0 -> x1, local copies, waits for them, and re-layouts: none -> 2.93 us  [shards(): everything = jnp.concatenate(r2, 0)]
  transfers between devices with their start and end apart: 3 -> 3, of which waited for: 2 -> 2; matrix products, arithmetic and copies ran while one was open for 23% -> 21% of each run, Pallas kernels for 0% -> 0%
where the time goes in v1:
time: 193 us; the launch traced here: 192 us
  waiting for transfers between devices  85.8 us (44%)
  other arithmetic  60.5 us (31%)
  local copies, waits for them, and re-layouts  16.9 us (9%)
  between operations  13.6 us (7%)
  starting transfers between devices  9.93 us (5%)
  matrix products  5.69 us (3%)
    all_to_all x1, waiting for transfers between devices, shards(): r2 = lax.all_to_all(u_next, axis_name='chan', split_axis=0, concat_axis=0)  44.2 us
    reduce_scatter x1, waiting for transfers between devices, shards(): lax.psum_scatter(correlate(receivers[:, None], sources, factor), 'tm', sc...  41.6 us
    convert_element_type x1, other arithmetic, transform_table(): cosine = jnp.cos(angles).astype(jnp.bfloat16)  35 us
    convert_element_type x1, other arithmetic, apply_filter(): return summed.astype(jnp.bfloat16)  18 us
    dot_general x1, matrix products, shards(): jnp.dot(windows, transform_table(), preferred_element_type=jnp.float32)  5.69 us
    all_to_all x1, starting transfers between devices, shards(): r2 = lax.all_to_all(u_next, axis_name='chan', split_axis=0, concat_axis=0)  5.01 us
    ppermute x1, starting transfers between devices, from_behind(): return lax.ppermute(block, axis, route)  4.89 us
  transfers between devices with their start and end apart: 3, of which 2 were waited for; matrix products, arithmetic and copies ran while one was open for 21% of the time, Pallas kernels for 0%

profile of v1, /device:TPU:0, one launch (start us, length us, event | category | flops | bytes accessed | tf_op | source)
XLA Modules:
  0.0 192.4 jit_solution(9648327893744761658)
XLA Ops:
  6.5 1.1 slice.239
  7.6 4.9 %collective-permute-start = (bf16[64,2080]{1,0:T(8,128)(2,1)S(1)}, bf16[64,2080]{1,0:T(8,128)(2,1)S(1)}, u32[]{:S(2)}, u32[]{:S(2)}) collective-permute-start(bf16[64,2080]{1,0:T(8,128)(2,1)S(1)} %slice.239), channel_id=1, source_target_pairs={{0,1},{2,3},{4,5},{6,7},{8,9},{10,11},{12,13},{14,15},{16,17},{18,... | collective-permute-start | bytes 798728 | tf_op jit(solution)/shard_map/ppermute | solution.py:16
  12.5 1.0 slice_bitcast_fusion.33
  13.5 35.0 %cosine_convert_fusion = (bf16[4096,512]{1,0:T(8,128)(2,1)}, bf16[4096,512]{1,0:T(8,128)(2,1)}) fusion(s32[512]{0:T(512)S(1)} %iota_add_fusion), kind=kLoop, calls=%fused_computation.14 | loop fusion | flops 35651584 | bytes 8390656 | tf_op jit(solution)/shard_map/convert_element_type | solution.py:24
  48.5 0.7 fusion.51
  49.3 1.0 slice_bitcast_fusion.34
  50.3 0.3 maximum_convert_fusion
  50.6 18.0 %fusion.11 = bf16[64,8192]{1,0:T(8,128)(2,1)S(1)} fusion(f32[64,8224]{1,0:T(8,128)S(1)} %maximum_convert_fusion, f32[64]{0:T(128)S(1)} %get-tuple-element.48, f32[64]{0:T(128)S(1)} %get-tuple-element.49, f32[64]{0:T(128)S(1)} %get-tuple-element.18, f32[64]{0:T(128)S(1)} %get-tuple-element.19, f32[64]{0:T(128)S(1)} %get-tuple-element.20, ...), kind=kLoop, calls=%fused_computation.23 | loop fusion | flops 34603008 | bytes 70263040 | tf_op jit(solution)/shard_map/convert_element_type | solution.py:40
  68.5 0.8 reshape.258
  69.3 1.3 fusion.58
  70.6 1.5 pad_maximum_fusion
  72.1 2.5 %reshape.259 = bf16[192,4096]{1,0:T(8,128)(2,1)} reshape(bf16[64,3,4096]{2,1,0:T(4,128)(2,1)S(1)} %pad_maximum_fusion) | data formatting | bytes 3145728 | tf_op jit(solution)/shard_map/reshape | solution.py:96
  74.6 5.7 %fusion.3 = f32[192,1024]{1,0:T(8,128)S(1)} fusion(bf16[192,4096]{1,0:T(8,128)(2,1)} %reshape.259, bf16[4096,512]{1,0:T(8,128)(2,1)} %get-tuple-element.51, bf16[4096,512]{1,0:T(8,128)(2,1)} %get-tuple-element.50), kind=kOutput, calls=%fused_computation.9 | convolution fusion | flops 1627389952 | bytes 10747904 | tf_op jit(solution)/shard_map/dot_general | solution.py:97
  80.3 0.1 fusion.57
  80.5 0.5 multiply_convert_fusion.1
  81.0 0.1 concatenate.39
  81.3 0.2 pad_maximum_fusion.1
  81.5 0.8 gather_fusion
  82.4 1.5 stack.2
  84.0 5.0 %all-to-all-start = ((bf16[8,36,3,1024]{3,1,2,0:T(8,128)(2,1)}), bf16[8,36,3,1024]{3,1,2,0:T(8,128)(2,1)S(1)}, u32[]{:S(2)}, u32[]{:S(2)}) async-start(bf16[8,36,3,1024]{3,1,2,0:T(8,128)(2,1)} %stack.2), calls=%async_computation | async-start | bytes 3932160 | tf_op jit(solution)/shard_map/all_to_all | solution.py:107
  89.0 0.2 reduce-window.9
  89.3 0.7 gather_fusion.1
  90.2 0.3 maximum_convert_fusion.1
  90.5 0.2 slice_bitcast_fusion.1
  90.7 0.1 copy.17
  90.9 0.1 copy.18
  91.0 44.2 %all-to-all-done = bf16[8,36,3,1024]{3,1,2,0:T(8,128)(2,1)S(1)} async-done(((bf16[8,36,3,1024]{3,1,2,0:T(8,128)(2,1)}), bf16[8,36,3,1024]{3,1,2,0:T(8,128)(2,1)S(1)}, u32[]{:S(2)}, u32[]{:S(2)}) %all-to-all-start) | async-done | bytes 1769504 | tf_op jit(solution)/shard_map/all_to_all | solution.py:107
  135.2 2.9 %copy.19 = bf16[8,36,3,1024]{3,2,1,0:T(4,128)(2,1)} copy(bf16[8,36,3,1024]{3,1,2,0:T(8,128)(2,1)S(1)} %all-to-all-done) | data formatting | bytes 3538944 | tf_op jit(solution)/shard_map/reshape | solution.py:108
  138.1 2.3 %gather_fusion.2 = bf16[12,3,1024]{2,1,0:T(4,128)(2,1)S(1)} fusion(bf16[288,3,1024]{2,1,0:T(4,128)(2,1)} %bitcast.96, s32[1024]{0:T(1024)S(1)} %pad_clamp_fusion), kind=kCustom, calls=%fused_computation.2 | custom fusion | bytes 147504 | tf_op jit(solution)/shard_map/gather | solution.py:109
  140.4 1.4 add_reduce_fusion
  141.9 2.1 %maximum_multiply_fusion = f32[64,12,1024]{2,0,1:T(8,128)} fusion(f32[64,12,512]{2,0,1:T(8,128)S(1)} %get-tuple-element.6, f32[64,12,512]{2,0,1:T(8,128)S(1)} %get-tuple-element.5), kind=kLoop, calls=%fused_computation.20 | loop fusion | flops 1572864 | bytes 6291456 | tf_op jit(solution)/shard_map/mul | solution.py:76
  144.0 41.6 %reduce-scatter.2.cloned.1.call-done = f32[32,12,1024]{2,0,1:T(8,128)} async-done(((f32[64,12,1024]{2,0,1:T(8,128)}), f32[32,12,1024]{2,0,1:T(8,128)}) %reduce-scatter.2.cloned.1.call-update) | async-done | bytes 1572880 | tf_op jit(solution)/shard_map/reduce_scatter | solution.py:117
  (24 shorter events, 0.7 us)
Async XLA Ops:
  7.6 42.6 %collective-permute-start = (bf16[64,2080]{1,0:T(8,128)(2,1)S(1)}, bf16[64,2080]{1,0:T(8,128)(2,1)S(1)}, u32[]{:S(2)}, u32[]{:S(2)}) collective-permute-start(bf16[64,2080]{1,0:T(8,128)(2,1)S(1)} %slice.239), channel_id=1, source_target_pairs={{0,1},{2,3},{4,5},{6,7},{8,9},{10,11},{12,13},{14,15},{16,17},{18,... | collective-permute-start | bytes 798728 | tf_op jit(solution)/shard_map/ppermute | solution.py:16
  13.5 36.8 %copy-start = (bf16[64,6144]{1,0:T(8,128)(2,1)S(1)}, bf16[64,6144]{1,0:T(8,128)(2,1)}, u32[]{:S(2)}) copy-start(bf16[64,6144]{1,0:T(8,128)(2,1)} %param.5) | copy-start | bytes 2359300
  84.0 5.1 %copy-start.2 = (s32[8]{0:T(128)S(1)}, s32[8]{0:T(128)}, u32[]{:S(2)}) copy-start(s32[8]{0:T(128)} %param.7) | copy-start | bytes 100
  84.0 5.3 %copy-start.1 = (s32[1,12]{1,0:T(1,128)S(1)}, s32[1,12]{1,0:T(1,128)}, u32[]{:S(2)}) copy-start(s32[1,12]{1,0:T(1,128)} %param.9) | copy-start | bytes 148
  84.0 51.2 %all-to-all-start = ((bf16[8,36,3,1024]{3,1,2,0:T(8,128)(2,1)}), bf16[8,36,3,1024]{3,1,2,0:T(8,128)(2,1)S(1)}, u32[]{:S(2)}, u32[]{:S(2)}) async-start(bf16[8,36,3,1024]{3,1,2,0:T(8,128)(2,1)} %stack.2), calls=%async_computation | async-start | bytes 3932160 | tf_op jit(solution)/shard_map/all_to_all | solution.py:107
  89.0 96.6 %reduce-scatter.2.cloned.1.call-start = ((), (), s32[]{:S(2)}) async-start(), calls=%async_computation.2 | async-start | bytes 4718592 | tf_op jit(solution)/shard_map/reduce_scatter | solution.py:117
Sparse Core Ops, SparseCore 0:
  144.1 41.4 reduce-scatter.1
